TPU v7x, 1024 devices: a whole 4x4x32 slice. The times are simulated.
1024 devices in a mesh: rows: 64 (over z_lo, x), filt: 16 (over y, z_hi, core).
Axes of the slice: x: 4, y: 4, z: 32 (z_hi: 2, z_lo: 16; z = z_hi * 16 + z_lo), core: 2. Of those that a mesh axis runs over, the one named last changes fastest.
Arguments:
- features: bfloat16 [768, 48, 2048], P('rows'), may hold values from -6 to 6
- point_weight: bfloat16 [2048, 256], P(None, 'filt'), may hold values from -0.125 to 0.125
- dilated_weight: bfloat16 [3, 3, 3, 2048, 256], P(None, None, None, None, 'filt'), may hold values from -0.046875 to 0.046875
- branch_bias: float32 [4, 256], P(None, 'filt'), may hold values from -3 to 3
- project_weight: bfloat16 [4, 256, 256], replicated, may hold values from -0.1875 to 0.1875
- project_bias: float32 [256], replicated, may hold values from -3 to 3
- cotangent: bfloat16 [768, 48, 256], P('rows'), may hold values from -6 to 6
Outputs:
- head_output: bfloat16 [768, 48, 256], P('rows', None, 'filt')
- feature_grad: bfloat16 [768, 48, 2048], P('rows', None, 'filt')
All inputs are finite; a program needn't handle non-finite values.
Results may differ from a plain program's by a relative error of at most 0.035.
The roundings to bfloat16 on the way count: a program that leaves them out, or rounds other values in their place, can miss the bound.
Values may be sent and summed in bfloat16 or wider, within the bound.
A program may use at most 128 MiB of HBM per device.

v0:
```python
import jax
import jax.numpy as jnp
from jax import lax
from jax.sharding import PartitionSpec as P

FIRST_DILATION = 12
SECOND_DILATION = 24
THIRD_DILATION = 36


def passed_along(x, axis, by):
    devices = lax.axis_size(axis)
    pairs = [(i, i + by) for i in range(devices) if 0 <= i + by < devices]
    return lax.ppermute(x, axis, pairs)


def shift_columns(field, amount):
    breadth = field.shape[1]
    if amount == 0:
        return field
    padding = [(0, 0)] * field.ndim
    if amount > 0:
        kept = field[:, amount:]
        padding[1] = (0, amount)
    else:
        kept = field[:, : breadth + amount]
        padding[1] = (-amount, 0)
    return jnp.pad(kept, padding)


def fetch_sums(field, offset):
    return passed_along(field, "rows", offset)


def fetch_grads(field, offset):
    return passed_along(field, "rows", offset)


def shift_rows(field, amount, fetcher):
    height = field.shape[0]
    quotient = amount // height

    def extract_block(offset):
        if offset == 0:
            return field
        return fetcher(field, offset)

    return extract_block(quotient)


def make_kernel_taps(variants, dilation_rates):
    stacked = [variants[:, :, 0]]
    for branch, dilation in enumerate(dilation_rates):
        for row_tap in range(3):
            source = variants[:, :, 1 + 3 * branch + row_tap]
            for col_tap in range(3):
                stacked.append(shift_columns(source, -(col_tap - 1) * dilation))
    return jnp.stack(stacked, 2)


def on_device(
    features, point_weight, dilated_weight, branch_bias, project_weight, project_bias, cotangent
):
    height, breadth, channels = features.shape
    pixels = height * breadth
    own_width = point_weight.shape[1]
    filters = lax.axis_size("filt")
    member = lax.axis_index("filt")
    branch_outputs = project_weight.shape[2]
    own_out = branch_outputs // filters
    own_channels = channels // filters
    dilation_rates = (FIRST_DILATION, SECOND_DILATION, THIRD_DILATION)
    all_weights = jnp.concatenate(
        [point_weight[None], dilated_weight.reshape(27, channels, own_width)], 0
    )
    flattened = features.reshape(pixels, channels)
    tap_terms = jnp.einsum(
        "pc,tco->pto", flattened, all_weights, preferred_element_type=jnp.float32
    )
    tap_terms = tap_terms.reshape(height, breadth, 28, own_width)
    pre_list = [tap_terms[:, :, 0, :] + branch_bias[0]]
    for branch, dilation in enumerate(dilation_rates):
        summed_result = jnp.zeros((height, breadth, own_width), jnp.float32)
        for row_tap in range(3):
            row_sum = jnp.zeros((height, breadth, own_width), jnp.float32)
            for col_tap in range(3):
                row_sum = row_sum + shift_columns(
                    tap_terms[:, :, 1 + 9 * branch + 3 * row_tap + col_tap, :],
                    (col_tap - 1) * dilation,
                )
            summed_result = summed_result + shift_rows(
                row_sum, -(row_tap - 1) * dilation, fetch_sums
            )
        pre_list.append(summed_result + branch_bias[branch + 1])
    branch_pre = jnp.stack(pre_list, 2)
    activations = jnp.maximum(branch_pre, 0.0).astype(jnp.bfloat16).reshape(pixels, 4 * own_width)
    grouped = project_weight.reshape(4, filters, own_width, branch_outputs)
    own_rows = lax.dynamic_index_in_dim(grouped, member, 1, keepdims=False).reshape(
        4 * own_width, branch_outputs
    )
    flat_cotangent = cotangent.reshape(pixels, branch_outputs)
    ordered = jnp.transpose(grouped, (1, 0, 2, 3)).reshape(filters * 4 * own_width, branch_outputs)
    project_pre = jnp.dot(
        lax.all_gather(activations, "filt", axis=1, tiled=True),
        ordered,
        preferred_element_type=jnp.float32,
    )
    project_pre = project_pre + project_bias
    head_grad = jnp.where(project_pre > 0, flat_cotangent.astype(jnp.float32), 0.0).astype(
        jnp.bfloat16
    )
    own_pre = lax.dynamic_slice_in_dim(project_pre, member * own_out, own_out, 1)
    act_grad = jnp.dot(head_grad, own_rows.T, preferred_element_type=jnp.float32)
    head_output = jnp.maximum(own_pre, 0.0).astype(jnp.bfloat16).reshape(height, breadth, own_out)
    branch_grad = jnp.where(
        branch_pre > 0, act_grad.reshape(height, breadth, 4, own_width), 0.0
    ).astype(jnp.bfloat16)
    variant_list = [branch_grad[:, :, 0, :]]
    for branch, dilation in enumerate(dilation_rates):
        for row_tap in range(3):
            variant_list.append(
                shift_rows(branch_grad[:, :, branch + 1, :], (row_tap - 1) * dilation, fetch_grads)
            )
    variants = jnp.stack(variant_list, 2)
    stacked = make_kernel_taps(variants, dilation_rates).reshape(pixels, 28, own_width)
    input_grad = lax.psum_scatter(
        jnp.einsum("pto,tco->cp", stacked, all_weights, preferred_element_type=jnp.float32),
        "filt",
        scatter_dimension=0,
        tiled=True,
    ).T
    feature_grad = input_grad.astype(jnp.bfloat16).reshape(height, breadth, own_channels)
    return (head_output, feature_grad)


def solution(mesh):
    in_specs = (
        P("rows", None, None),
        P(None, "filt"),
        P(None, None, None, None, "filt"),
        P(None, "filt"),
        P(),
        P(),
        P("rows", None, None),
    )
    out_specs = (P("rows", None, "filt"), P("rows", None, "filt"))
    return jax.shard_map(
        on_device, mesh=mesh, in_specs=in_specs, out_specs=out_specs, check_vma=False
    )
```

profile of v0, /device:TPU:2, one launch (start us, length us, event | category | flops | bytes accessed | tf_op | source)
XLA Modules:
  0.0 506.1 jit_solution(11978105642348974208)
XLA Ops:
  7.2 1.6 copy-done
  8.8 3.1 convolution_bitcast_fusion.1
  11.9 2.9 reshape.99
  14.9 2.0 fusion.37
  17.1 4.0 collective-permute-start.2
  21.4 1.3 collective-permute-start.3
  23.0 6.7 %collective-permute-start.4 = (f32[12,48,16]{1,2,0:T(8,128)S(1)}, f32[12,48,16]{1,2,0:T(8,128)S(1)}, u32[]{:S(2)}, u32[]{:S(2)}) collective-permute-start(f32[12,48,16]{1,2,0:T(8,128)S(1)} %fusion.11), channel_id=1, source_target_pairs={{0,48},{16,64},{32,80},{48,96},{64,112},{80,128},{96,144},{112,160... | collective-permute-start | bytes 110600 | tf_op jit(solution)/shard_map/ppermute | solution.py:14
  29.7 1.4 fusion.38
  31.4 1.3 collective-permute-start.5
  33.0 9.0 %collective-permute-start = (f32[12,48,16]{1,2,0:T(8,128)S(1)}, f32[12,48,16]{1,2,0:T(8,128)S(1)}, u32[]{:S(2)}, u32[]{:S(2)}) collective-permute-start(f32[12,48,16]{1,2,0:T(8,128)S(1)} %fusion.31), channel_id=1, source_target_pairs={{0,16},{16,32},{32,48},{48,64},{64,80},{80,96},{96,112},{112,128},... | collective-permute-start | bytes 110600 | tf_op jit(solution)/shard_map/ppermute | solution.py:14
  42.8 2.1 collective-permute-start.1
  45.2 4.3 collective-permute-done.1
  49.6 0.6 copy-done.6
  50.5 0.8 convert_element_type.77
  51.4 136.8 %all-gather.2.cloned.1.call-done = bf16[576,1024]{0,1:T(8,128)(2,1)} async-done(((bf16[576,64]{0,1:T(8,128)(2,1)}), bf16[576,1024]{0,1:T(8,128)(2,1)}) %all-gather.2.cloned.1.call-update) | async-done | bytes 1179664 | tf_op jit(solution)/shard_map/all_gather | solution.py:104
  188.3 2.7 fusion.1
  191.3 2.5 collective-permute-start.6
  193.9 3.4 collective-permute-start.7
  197.2 1.3 collective-permute-start.8
  198.6 6.7 %collective-permute-start.9 = (bf16[12,48,16]{1,2,0:T(8,128)(2,1)S(1)}, bf16[12,48,16]{1,2,0:T(8,128)(2,1)S(1)}, u32[]{:S(2)}, u32[]{:S(2)}) collective-permute-start(bf16[12,48,16]{1,2,0:T(8,128)(2,1)S(1)} %get-tuple-element.38), channel_id=1, source_target_pairs={{0,32},{16,48},{32,64},{48,80},{64,96},{80,112},{96,128},{112,144}... | collective-permute-start | bytes 55304 | tf_op jit(solution)/shard_map/ppermute | solution.py:14
  205.4 1.3 collective-permute-start.10
  206.9 0.6 constant_dynamic-update-slice_fusion.27
  209.1 5.4 %collective-permute-start.11 = (bf16[12,48,16]{1,2,0:T(8,128)(2,1)S(1)}, bf16[12,48,16]{1,2,0:T(8,128)(2,1)S(1)}, u32[]{:S(2)}, u32[]{:S(2)}) collective-permute-start(bf16[12,48,16]{1,2,0:T(8,128)(2,1)S(1)} %get-tuple-element.39), channel_id=1, source_target_pairs={{0,48},{16,64},{32,80},{48,96},{64,112},{80,128},{96,144},{112,160... | collective-permute-start | bytes 55304 | tf_op jit(solution)/shard_map/ppermute | solution.py:14
  218.3 0.6 constant_dynamic-update-slice_fusion.26
  218.9 0.6 constant_dynamic-update-slice_fusion.25
  219.6 0.6 constant_dynamic-update-slice_fusion.24
  220.8 0.6 constant_dynamic-update-slice_fusion.22
  221.4 0.6 constant_dynamic-update-slice_fusion.21
  222.0 0.6 constant_dynamic-update-slice_fusion.20
  222.6 0.6 constant_dynamic-update-slice_fusion.19
  223.8 0.6 constant_dynamic-update-slice_fusion.17
  224.4 0.6 constant_dynamic-update-slice_fusion.16
  225.6 0.6 constant_dynamic-update-slice_fusion.14
  226.2 0.6 constant_dynamic-update-slice_fusion.13
  227.4 0.6 constant_dynamic-update-slice_fusion.11
  228.1 0.6 constant_dynamic-update-slice_fusion.10
  228.7 0.6 constant_dynamic-update-slice_fusion.9
  229.9 0.6 constant_dynamic-update-slice_fusion.7
  231.7 0.6 constant_dynamic-update-slice_fusion.4
  232.3 0.6 constant_dynamic-update-slice_fusion.3
  232.9 0.6 constant_dynamic-update-slice_fusion.2
  233.5 0.6 constant_dynamic-update-slice_fusion.1
  234.1 0.6 constant_dynamic-update-slice_fusion
  234.7 5.2 %convolution_bitcast_fusion = f32[2048,576]{0,1:T(8,128)} fusion(bf16[576,28,16]{0,2,1:T(8,128)(2,1)} %constant_dynamic-update-slice_fusion, bf16[27,2048,16]{1,2,0:T(8,128)(2,1)} %bitcast.259, bf16[1,2048,16]{1,2,0:T(8,128)(2,1)S(1)} %bitcast.261), kind=kOutput, calls=%fused_computation | convolution fusion | flops 1057882112 | bytes 7069696 | tf_op jit(solution)/shard_map/pto,tco->cp/dot_general | solution.py:127
  239.9 0.9 copy-done.8
  241.0 0.7 copy.185
  241.7 255.9 %reduce-scatter.2.cloned.1.call-done = f32[128,576]{0,1:T(8,128)} async-done(((f32[2048,576]{0,1:T(8,128)}), f32[128,576]{0,1:T(8,128)}) %reduce-scatter.2.cloned.1.call-update) | async-done | bytes 294928 | tf_op jit(solution)/shard_map/reduce_scatter | solution.py:126
  497.6 1.6 convert_element_type.83
  (163 shorter events, 12.8 us)
Async XLA Ops:
  7.2 1.7 copy-start
  7.2 181.1 %all-gather.2.cloned.1.call-start = ((), (), s32[]{:S(2)}) async-start(), calls=%async_computation.1 | async-start | bytes 1392640 | tf_op jit(solution)/shard_map/all_gather | solution.py:104
  17.1 25.8 %collective-permute-start.2 = (f32[12,48,16]{1,2,0:T(8,128)S(1)}, f32[12,48,16]{1,2,0:T(8,128)S(1)}, u32[]{:S(2)}, u32[]{:S(2)}) collective-permute-start(f32[12,48,16]{1,2,0:T(8,128)S(1)} %fusion.21), channel_id=1, source_target_pairs={{0,32},{16,48},{32,64},{48,80},{64,96},{80,112},{96,128},{112,144}... | collective-permute-start | bytes 110600 | tf_op jit(solution)/shard_map/ppermute | solution.py:14
  21.4 23.5 %collective-permute-start.3 = (f32[12,48,16]{1,2,0:T(8,128)S(1)}, f32[12,48,16]{1,2,0:T(8,128)S(1)}, u32[]{:S(2)}, u32[]{:S(2)}) collective-permute-start(f32[12,48,16]{1,2,0:T(8,128)S(1)} %fusion.13), channel_id=1, source_target_pairs={{32,0},{48,16},{64,32},{80,48},{96,64},{112,80},{128,96},{144,112}... | collective-permute-start | bytes 110600 | tf_op jit(solution)/shard_map/ppermute | solution.py:14
  23.0 19.0 %copy-start.9 = (f32[4,16]{1,0:T(4,128)S(1)}, f32[4,16]{1,0:T(4,128)}, u32[]{:S(2)}) copy-start(f32[4,16]{1,0:T(4,128)} %param.10) | copy-start | bytes 772
  23.0 22.1 %collective-permute-start.4 = (f32[12,48,16]{1,2,0:T(8,128)S(1)}, f32[12,48,16]{1,2,0:T(8,128)S(1)}, u32[]{:S(2)}, u32[]{:S(2)}) collective-permute-start(f32[12,48,16]{1,2,0:T(8,128)S(1)} %fusion.11), channel_id=1, source_target_pairs={{0,48},{16,64},{32,80},{48,96},{64,112},{80,128},{96,144},{112,160... | collective-permute-start | bytes 110600 | tf_op jit(solution)/shard_map/ppermute | solution.py:14
  31.4 13.6 %collective-permute-start.5 = (f32[12,48,16]{1,2,0:T(8,128)S(1)}, f32[12,48,16]{1,2,0:T(8,128)S(1)}, u32[]{:S(2)}, u32[]{:S(2)}) collective-permute-start(f32[12,48,16]{1,2,0:T(8,128)S(1)} %fusion.3), channel_id=1, source_target_pairs={{48,0},{64,16},{80,32},{96,48},{112,64},{128,80},{144,96},{160,112... | collective-permute-start | bytes 110600 | tf_op jit(solution)/shard_map/ppermute | solution.py:14
  33.0 12.2 %collective-permute-start = (f32[12,48,16]{1,2,0:T(8,128)S(1)}, f32[12,48,16]{1,2,0:T(8,128)S(1)}, u32[]{:S(2)}, u32[]{:S(2)}) collective-permute-start(f32[12,48,16]{1,2,0:T(8,128)S(1)} %fusion.31), channel_id=1, source_target_pairs={{0,16},{16,32},{32,48},{48,64},{64,80},{80,96},{96,112},{112,128},... | collective-permute-start | bytes 110600 | tf_op jit(solution)/shard_map/ppermute | solution.py:14
  42.7 8.6 %copy-start.1 = (bf16[4,256,256]{2,1,0:T(8,128)(2,1)S(1)}, bf16[4,256,256]{2,1,0:T(8,128)(2,1)}, u32[]{:S(2)}) copy-start(bf16[4,256,256]{2,1,0:T(8,128)(2,1)} %param.11) | copy-start | bytes 1572868
  42.8 6.6 %collective-permute-start.1 = (f32[12,48,16]{1,2,0:T(8,128)S(1)}, f32[12,48,16]{1,2,0:T(8,128)S(1)}, u32[]{:S(2)}, u32[]{:S(2)}) collective-permute-start(f32[12,48,16]{1,2,0:T(8,128)S(1)} %fusion.23), channel_id=1, source_target_pairs={{16,0},{32,16},{48,32},{64,48},{80,64},{96,80},{112,96},{128,112},... | collective-permute-start | bytes 110600 | tf_op jit(solution)/shard_map/ppermute | solution.py:14
  45.0 4.6 copy-start.2
  45.1 143.2 %copy-start.11 = (f32[256]{0:T(256)S(1)}, f32[256]{0:T(256)}, u32[]{:S(2)}) copy-start(f32[256]{0:T(256)} %param.12) | copy-start | bytes 3076
  45.2 4.4 copy-start.4
  49.6 0.6 copy-start.6
  51.3 446.3 %reduce-scatter.2.cloned.1.call-start = ((), (), s32[]{:S(2)}) async-start(), calls=%async_computation.2 | async-start | bytes 5013504 | tf_op jit(solution)/shard_map/reduce_scatter | solution.py:126
  188.2 2.7 copy-start.3
  188.2 2.7 copy-start.5
  188.2 2.7 copy-start.7
  191.3 17.8 %collective-permute-start.6 = (bf16[12,48,16]{1,2,0:T(8,128)(2,1)S(1)}, bf16[12,48,16]{1,2,0:T(8,128)(2,1)S(1)}, u32[]{:S(2)}, u32[]{:S(2)}) collective-permute-start(bf16[12,48,16]{1,2,0:T(8,128)(2,1)S(1)} %get-tuple-element.37), channel_id=1, source_target_pairs={{16,0},{32,16},{48,32},{64,48},{80,64},{96,80},{112,96},{128,112},... | collective-permute-start | bytes 55304 | tf_op jit(solution)/shard_map/ppermute | solution.py:14
  193.9 20.8 %collective-permute-start.7 = (bf16[12,48,16]{1,2,0:T(8,128)(2,1)S(1)}, bf16[12,48,16]{1,2,0:T(8,128)(2,1)S(1)}, u32[]{:S(2)}, u32[]{:S(2)}) collective-permute-start(bf16[12,48,16]{1,2,0:T(8,128)(2,1)S(1)} %get-tuple-element.37), channel_id=1, source_target_pairs={{0,16},{16,32},{32,48},{48,64},{64,80},{80,96},{96,112},{112,128},... | collective-permute-start | bytes 55304 | tf_op jit(solution)/shard_map/ppermute | solution.py:14
  197.2 17.5 %collective-permute-start.8 = (bf16[12,48,16]{1,2,0:T(8,128)(2,1)S(1)}, bf16[12,48,16]{1,2,0:T(8,128)(2,1)S(1)}, u32[]{:S(2)}, u32[]{:S(2)}) collective-permute-start(bf16[12,48,16]{1,2,0:T(8,128)(2,1)S(1)} %get-tuple-element.38), channel_id=1, source_target_pairs={{32,0},{48,16},{64,32},{80,48},{96,64},{112,80},{128,96},{144,112}... | collective-permute-start | bytes 55304 | tf_op jit(solution)/shard_map/ppermute | solution.py:14
  198.6 16.2 %collective-permute-start.9 = (bf16[12,48,16]{1,2,0:T(8,128)(2,1)S(1)}, bf16[12,48,16]{1,2,0:T(8,128)(2,1)S(1)}, u32[]{:S(2)}, u32[]{:S(2)}) collective-permute-start(bf16[12,48,16]{1,2,0:T(8,128)(2,1)S(1)} %get-tuple-element.38), channel_id=1, source_target_pairs={{0,32},{16,48},{32,64},{48,80},{64,96},{80,112},{96,128},{112,144}... | collective-permute-start | bytes 55304 | tf_op jit(solution)/shard_map/ppermute | solution.py:14
  205.4 9.6 %collective-permute-start.10 = (bf16[12,48,16]{1,2,0:T(8,128)(2,1)S(1)}, bf16[12,48,16]{1,2,0:T(8,128)(2,1)S(1)}, u32[]{:S(2)}, u32[]{:S(2)}) collective-permute-start(bf16[12,48,16]{1,2,0:T(8,128)(2,1)S(1)} %get-tuple-element.39), channel_id=1, source_target_pairs={{48,0},{64,16},{80,32},{96,48},{112,64},{128,80},{144,96},{160,112... | collective-permute-start | bytes 55304 | tf_op jit(solution)/shard_map/ppermute | solution.py:14
  209.1 8.6 %collective-permute-start.11 = (bf16[12,48,16]{1,2,0:T(8,128)(2,1)S(1)}, bf16[12,48,16]{1,2,0:T(8,128)(2,1)S(1)}, u32[]{:S(2)}, u32[]{:S(2)}) collective-permute-start(bf16[12,48,16]{1,2,0:T(8,128)(2,1)S(1)} %get-tuple-element.39), channel_id=1, source_target_pairs={{0,48},{16,64},{32,80},{48,96},{64,112},{80,128},{96,144},{112,160... | collective-permute-start | bytes 55304 | tf_op jit(solution)/shard_map/ppermute | solution.py:14
  216.7 18.0 %copy-start.10 = (bf16[2048,16]{0,1:T(8,128)(2,1)S(1)}, bf16[2048,16]{0,1:T(8,128)(2,1)}, u32[]{:S(2)}) copy-start(bf16[2048,16]{0,1:T(8,128)(2,1)} %param.8) | copy-start | bytes 196612
  239.9 1.0 copy-start.8
Sparse Core Ops, SparseCore 0:
  51.4 136.7 all-gather.1
  240.1 257.5 reduce-scatter.1
where the time goes:
time: 507 us; the launch traced here: 506 us
  waiting for transfers between devices  397 us (78%)
  starting transfers between devices  45.1 us (9%)
  local copies, waits for them, and re-layouts  35 us (7%)
  between operations  14.9 us (3%)
  matrix products  11.3 us (2%)
    reduce_scatter x1, waiting for transfers between devices, on_device(): lax.psum_scatter(jnp.einsum('pto,tco->cp', stacked, all_weights, preferre...  256 us
    all_gather x1, waiting for transfers between devices, on_device(): lax.all_gather(activations, 'filt', axis=1, tiled=True)  137 us
    ppermute x12, starting transfers between devices, passed_along(): return lax.ppermute(x, axis, pairs)  45 us
    unnamed x74, local copies, waits for them, and re-layouts  20.7 us
  transfers between devices with their start and end apart: 14, of which 3 were waited for; matrix products, arithmetic and copies ran while one was open for 2% of the time, Pallas kernels for 0%

commit v1 on v0

v1 whole, which is shorter than its diff:
```python
import jax
import jax.numpy as jnp
from jax import lax
from jax.experimental import pallas as pl
from jax.experimental.pallas import tpu as pltpu
from jax.sharding import PartitionSpec as P

FIRST_DILATION = 12
SECOND_DILATION = 24
THIRD_DILATION = 36
DILATIONS = (FIRST_DILATION, SECOND_DILATION, THIRD_DILATION)
ROW_BLOCKS = 64
HEIGHT = 12
BREADTH = 48
PIXELS = HEIGHT * BREADTH
LANES = 640
CHANNELS = 2048
OWN = 16
TAPS = 28
TERMS = TAPS * OWN
MEMBERS = 16
OUTPUTS = 256
BLOCK = 128
PIECE_ROWS = TERMS // 4
PIECE_LANES = 256
MESH = pl.DeviceIdType.MESH
BF16 = jnp.bfloat16
F32 = jnp.float32


def device(x, y, z, core):
    x, y, z = lax.rem(x + 4, 4), lax.rem(y + 4, 4), lax.rem(z + 32, 32)
    return (lax.rem(z, 16) * 4 + x, (y * 2 + z // 16) * 2 + core)


def remote(source, target, send_sem, recv_sem, where):
    return pltpu.make_async_remote_copy(
        src_ref=source,
        dst_ref=target,
        send_sem=send_sem,
        recv_sem=recv_sem,
        device_id=where,
        device_id_type=MESH,
    )


def kernel(
    x_hbm, dilated_hbm, point_hbm, project_hbm, cot_hbm, bias_hbm, project_bias_hbm,
    head_ref, grad_ref,
    bias_ref, project_bias_ref, x_buf, w_buf, w_both, project, project_t, cot_buf, cot_t, columns,
    taps, row_send, row_recv, acts, pre, grads, grad_recv, spread, spread_t,
    part, part_low, core_recv, sum_send, sum_recv,
    load_sem, fill_sem, row_ss, row_rs, act_ss, act_rs, first_ss, first_rs, zg_ss, zg_rs,
    xg_ss, xg_rs, grow_ss, grow_rs, core_ss, core_rs, sum_ss, sum_rs,
):
    row = lax.axis_index("rows")
    member = lax.axis_index("filt")
    x, z_low = lax.rem(row, 4), row // 4
    y, half, core = member // 4, lax.rem(member // 2, 2), lax.rem(member, 2)
    z = half * 16 + z_low
    z_quarter = lax.rem(z_low, 4)
    other = member + 2 - 4 * half
    twin = 1 - 2 * core

    def row_offset(slot):
        return (slot // 2 + 1) * (1 - 2 * (slot % 2))

    def sends(slot):
        place = row + row_offset(slot)
        return jnp.logical_and(place >= 0, place < ROW_BLOCKS)

    def gets(slot):
        place = row - row_offset(slot)
        return jnp.logical_and(place >= 0, place < ROW_BLOCKS)

    opposite = device(x, y, z + 16, core)
    eighth = device(x, y, z + jnp.where(z_low >= 8, 8, -8), core)
    partner = device(x, y, z, 1 - core)
    y_peers = [device(x, y + d, z, core) for d in (1, 3, 2)]
    y_members = [(lax.rem(y + d, 4) * 2 + half) * 2 + core for d in (1, 3, 2)]
    y_others = [(lax.rem(y + d, 4) * 2 + 1 - half) * 2 + core for d in (1, 3, 2)]
    z_base = z - z_quarter
    z_peers = [device(x, y, z_base + lax.rem(z_quarter + d, 4), core) for d in (1, 2, 3)]
    x_peers = [device(x + d, y, z, core) for d in (1, 2, 3)]

    barrier = pltpu.get_barrier_semaphore()
    fixed_peers = [opposite, eighth, partner] + y_peers + z_peers + x_peers
    for peer in fixed_peers:
        pl.semaphore_signal(barrier, inc=1, device_id=peer, device_id_type=MESH)
    heard = jnp.int32(len(fixed_peers))
    for slot in range(6):
        @pl.when(sends(slot))
        def _():
            pl.semaphore_signal(
                barrier, inc=1, device_id=(row + row_offset(slot), member), device_id_type=MESH
            )
        heard = heard + sends(slot).astype(jnp.int32)

    loads = [
        pltpu.make_async_copy(x_hbm, x_buf.at[pl.ds(0, PIXELS)], load_sem.at[0]),
        pltpu.make_async_copy(dilated_hbm, w_buf.at[pl.ds(0, TERMS - OWN)], load_sem.at[1]),
        pltpu.make_async_copy(point_hbm, w_buf.at[pl.ds(TERMS - OWN, OWN)], load_sem.at[2]),
        pltpu.make_async_copy(cot_hbm, cot_buf.at[pl.ds(0, PIXELS)], load_sem.at[3]),
    ] + [
        pltpu.make_async_copy(project_hbm.at[k], project.at[:, k], load_sem.at[4 + k])
        for k in range(4)
    ] + [
        pltpu.make_async_copy(bias_hbm, bias_ref, load_sem.at[8]),
        pltpu.make_async_copy(project_bias_hbm, project_bias_ref, load_sem.at[9]),
    ]
    for load in loads:
        load.start()
    x_buf[pl.ds(PIXELS, LANES - PIXELS), :] = jnp.zeros((LANES - PIXELS, CHANNELS), BF16)
    cot_buf[pl.ds(PIXELS, LANES - PIXELS), :] = jnp.zeros((LANES - PIXELS, OUTPUTS), BF16)
    for load in loads[:3]:
        load.wait()

    own_fill = []
    for block in range(4):
        lanes = pl.multiple_of(block * 512 + half * 256, 256)
        own_fill.append(
            pltpu.make_async_copy(
                w_buf.at[:, pl.ds(lanes, 256)],
                w_both.at[pl.ds(0, TERMS), pl.ds(block * 256, 256)],
                fill_sem.at[block],
            )
        )
    for fill in own_fill:
        fill.start()

    taps[...] = lax.dot_general(
        w_buf[...], x_buf[...], (((1,), (1,)), ((), ())), preferred_element_type=F32
    )

    column = lax.rem(lax.broadcasted_iota(jnp.int32, (1, LANES), 1), BREADTH)

    def shift_columns(field, amount):
        if amount == 0:
            return field
        inside = jnp.logical_and(column + amount >= 0, column + amount < BREADTH)
        return jnp.where(inside, pltpu.roll(field, (-amount) % LANES, 1), 0.0)

    def tap(k, i, j):
        return taps[pl.ds((9 * k + 3 * i + j) * OWN, OWN), :]

    def row_sum(k, i):
        d = DILATIONS[k]
        return (
            shift_columns(tap(k, i, 0), -d) + tap(k, i, 1) + shift_columns(tap(k, i, 2), d)
        )

    for k in range(3):
        row_send[2 * k] = row_sum(k, 0)
        row_send[2 * k + 1] = row_sum(k, 2)

    pl.semaphore_wait(barrier, heard)

    def row_copy(slot):
        return remote(
            row_send.at[slot], row_recv.at[slot], row_ss.at[slot], row_rs.at[slot],
            (row + row_offset(slot), member),
        )

    for slot in (4, 5, 2, 3, 0, 1):
        @pl.when(sends(slot))
        def _():
            row_copy(slot).start()

    z_rows = pl.multiple_of(z_quarter * PIECE_ROWS, 16)
    far_rows = pl.multiple_of(TERMS + z_quarter * PIECE_ROWS, 16)
    far_lanes = pl.multiple_of(x * PIECE_LANES, 128)
    give_lanes = pl.multiple_of(x * 512 + (1 - half) * 256, 256)
    first = remote(
        w_buf.at[pl.ds(z_rows, PIECE_ROWS), pl.ds(give_lanes, PIECE_LANES)],
        w_both.at[pl.ds(far_rows, PIECE_ROWS), pl.ds(far_lanes, PIECE_LANES)],
        first_ss.at[0], first_rs.at[0], eighth,
    )
    first.start()

    def diagonal(values, size):
        same = lax.broadcasted_iota(jnp.int32, (size, size), 0) == lax.broadcasted_iota(
            jnp.int32, (size, size), 1
        )
        return jnp.sum(
            jnp.where(same, jnp.broadcast_to(values, (size, size)), 0.0), axis=1, keepdims=True
        )

    for load in loads[8:]:
        load.wait()
    bias = bias_ref[...]
    biases = [diagonal(bias[k:k + 1, :], OWN) for k in range(4)]
    acts[member, pl.ds(0, OWN), :] = jnp.maximum(
        taps[pl.ds(TERMS - OWN, OWN), :] + biases[0], 0.0
    ).astype(BF16)
    centres = [row_sum(k, 1) + biases[k + 1] for k in range(3)]

    for k in range(3):
        total = centres[k]
        for slot in (2 * k, 2 * k + 1):
            @pl.when(gets(slot))
            def _():
                row_copy(slot).wait_recv()
            total = total + jnp.where(gets(slot), row_recv[slot], 0.0)
        acts[member, pl.ds((k + 1) * OWN, OWN), :] = jnp.maximum(total, 0.0).astype(BF16)

    started = []

    def pass_block(block, where):
        n = len(started)
        copy = remote(acts.at[block], acts.at[block], act_ss.at[n], act_rs.at[block], where)
        copy.start()
        started.append(copy)

    def await_block(block):
        remote(acts.at[block], acts.at[block], act_ss.at[0], act_rs.at[block], partner).wait_recv()

    pass_block(member, opposite)
    for peer in y_peers:
        pass_block(member, peer)
    pass_block(member, partner)

    for load in loads[3:8]:
        load.wait()
    project_rows = project[...].reshape(MEMBERS * 4 * OWN, OUTPUTS)
    project_t[...] = project_rows.T
    cot_t[...] = cot_buf[...].astype(F32).T
    columns[...] = jnp.broadcast_to(diagonal(project_bias_ref[...], OUTPUTS), (OUTPUTS, BLOCK))

    for n in range(3):
        await_block(y_members[n])
        pass_block(y_members[n], partner)

    def z_copy(d):
        return remote(
            w_both.at[pl.ds(far_rows, PIECE_ROWS), pl.ds(far_lanes, PIECE_LANES)],
            w_both.at[pl.ds(far_rows, PIECE_ROWS), pl.ds(far_lanes, PIECE_LANES)],
            zg_ss.at[d - 1], zg_rs.at[d - 1], z_peers[d - 1],
        )

    def x_copy(d, e):
        rows_from = pl.multiple_of(
            TERMS + lax.rem(z_quarter + 4 - d, 4) * PIECE_ROWS, 16
        )
        return remote(
            w_both.at[pl.ds(rows_from, PIECE_ROWS), pl.ds(far_lanes, PIECE_LANES)],
            w_both.at[pl.ds(rows_from, PIECE_ROWS), pl.ds(far_lanes, PIECE_LANES)],
            xg_ss.at[3 * d + e - 1], xg_rs.at[3 * d + e - 1], x_peers[e - 1],
        )

    first.wait_recv()
    for d in (1, 2, 3):
        z_copy(d).start()
    for e in (1, 2, 3):
        x_copy(0, e).start()

    await_block(other)
    for peer in y_peers:
        pass_block(other, peer)
    pass_block(other, partner)

    for d in (1, 2, 3):
        z_copy(d).wait_recv()
        for e in (1, 2, 3):
            x_copy(d, e).start()

    for n in range(3):
        await_block(y_others[n])
        pass_block(y_others[n], partner)
    for block in [member, other] + y_members + y_others:
        await_block(block + twin)

    pre[...] = (
        jnp.dot(
            project_t[...],
            acts[...].reshape(MEMBERS * 4 * OWN, LANES),
            preferred_element_type=F32,
        )
        + columns[:, 0:1]
    )
    head_grad = jnp.where(pre[...] > 0, cot_t[...], 0.0).astype(BF16)
    for side, block in ((0, member), (1, other)):
        act_grad = jnp.dot(
            project[block].reshape(4 * OWN, OUTPUTS), head_grad, preferred_element_type=F32
        )
        branch_grad = jnp.where(acts[block] > 0, act_grad, 0.0).astype(BF16)
        for k in range(4):
            grads[k, pl.ds(side * OWN, OWN), :] = branch_grad[k * OWN:(k + 1) * OWN]

    def grad_copy(slot):
        return remote(
            grads.at[slot // 2 + 1], grad_recv.at[slot], grow_ss.at[slot], grow_rs.at[slot],
            (row + row_offset(slot), member),
        )

    for slot in (4, 5, 2, 3, 0, 1):
        @pl.when(sends(slot))
        def _():
            grad_copy(slot).start()

    own_head = jnp.maximum(pre[pl.ds(pl.multiple_of(member * OWN, OWN), OWN), :], 0.0)
    for r in range(HEIGHT):
        head_ref[r] = own_head[:, r * BREADTH:(r + 1) * BREADTH].astype(BF16)

    def put(values, t):
        low = values.astype(BF16)
        for side in range(2):
            spread[pl.ds(side * TERMS + t * OWN, OWN), :] = low[side * OWN:(side + 1) * OWN]

    def put_columns(field, k, i):
        for j in range(3):
            put(shift_columns(field, -(j - 1) * DILATIONS[k]), 9 * k + 3 * i + j)

    put(grads[0].astype(F32), TAPS - 1)
    for k in range(3):
        put_columns(grads[k + 1].astype(F32), k, 1)
    for k in range(3):
        for slot, i in ((2 * k, 2), (2 * k + 1, 0)):
            @pl.when(gets(slot))
            def _():
                grad_copy(slot).wait_recv()
            put_columns(jnp.where(gets(slot), grad_recv[slot].astype(F32), 0.0), k, i)

    spread_t[...] = spread[...].T

    for fill in own_fill:
        fill.wait()
    for d in range(4):
        for e in (1, 2, 3):
            x_copy(d, e).wait_recv()

    def core_copy(n):
        return remote(
            part_low.at[n, 1 - core], core_recv.at[n], core_ss.at[n], core_rs.at[n], partner
        )

    order = (2, 1, 3, 0)
    for n, d in enumerate(order):
        lanes = pl.multiple_of(lax.rem(y + d, 4) * 256, 256)
        product = jnp.dot(
            spread_t[pl.ds(0, PIXELS), :], w_both[:, pl.ds(lanes, 256)], preferred_element_type=F32
        )
        for c in range(2):
            piece = product[:, c * BLOCK:(c + 1) * BLOCK]
            part[n, c] = piece
            part_low[n, c] = piece.astype(BF16)
        core_copy(n).start()

    def sum_copy(n):
        return remote(
            sum_send.at[n], sum_recv.at[n], sum_ss.at[n], sum_rs.at[n],
            device(x, y + order[n], z, core),
        )

    for n in range(3):
        core_copy(n).wait_recv()
        sum_send[n] = (part[n, core] + core_recv[n].astype(F32)).astype(BF16)
        sum_copy(n).start()
    core_copy(3).wait_recv()
    total = part[3, core] + core_recv[3].astype(F32)
    for n in range(3):
        sum_copy(n).wait_recv()
        total = total + sum_recv[n].astype(F32)
    grad_ref[...] = total.astype(BF16)

    for slot in range(6):
        @pl.when(sends(slot))
        def _():
            row_copy(slot).wait_send()
            grad_copy(slot).wait_send()
    first.wait_send()
    for copy in started:
        copy.wait_send()
    for d in (1, 2, 3):
        z_copy(d).wait_send()
    for d in range(4):
        for e in (1, 2, 3):
            x_copy(d, e).wait_send()
    for n in range(4):
        core_copy(n).wait_send()
    for n in range(3):
        sum_copy(n).wait_send()


def on_device(
    features, point_weight, dilated_weight, branch_bias, project_weight, project_bias, cotangent
):
    in_place = pl.BlockSpec(memory_space=pltpu.HBM)
    vmem = pl.BlockSpec(memory_space=pltpu.VMEM)
    dma = pltpu.SemaphoreType.DMA
    head, grad = pl.pallas_call(
        kernel,
        out_shape=(
            jax.ShapeDtypeStruct((HEIGHT, OWN, BREADTH), BF16),
            jax.ShapeDtypeStruct((PIXELS, BLOCK), BF16),
        ),
        in_specs=[in_place] * 7,
        out_specs=(vmem, vmem),
        scratch_shapes=[
            pltpu.VMEM((4, OWN), F32),
            pltpu.VMEM((1, OUTPUTS), F32),
            pltpu.VMEM((LANES, CHANNELS), BF16),
            pltpu.VMEM((TERMS, CHANNELS), BF16),
            pltpu.VMEM((2 * TERMS, CHANNELS // 2), BF16),
            pltpu.VMEM((MEMBERS, 4, OWN, OUTPUTS), BF16),
            pltpu.VMEM((OUTPUTS, MEMBERS * 4 * OWN), BF16),
            pltpu.VMEM((LANES, OUTPUTS), BF16),
            pltpu.VMEM((OUTPUTS, LANES), F32),
            pltpu.VMEM((OUTPUTS, BLOCK), F32),
            pltpu.VMEM((TERMS, LANES), F32),
            pltpu.VMEM((6, OWN, LANES), F32),
            pltpu.VMEM((6, OWN, LANES), F32),
            pltpu.VMEM((MEMBERS, 4 * OWN, LANES), BF16),
            pltpu.VMEM((OUTPUTS, LANES), F32),
            pltpu.VMEM((4, 2 * OWN, LANES), BF16),
            pltpu.VMEM((6, 2 * OWN, LANES), BF16),
            pltpu.VMEM((2 * TERMS, LANES), BF16),
            pltpu.VMEM((LANES, 2 * TERMS), BF16),
            pltpu.VMEM((4, 2, PIXELS, BLOCK), F32),
            pltpu.VMEM((4, 2, PIXELS, BLOCK), BF16),
            pltpu.VMEM((4, PIXELS, BLOCK), BF16),
            pltpu.VMEM((3, PIXELS, BLOCK), BF16),
            pltpu.VMEM((3, PIXELS, BLOCK), BF16),
            dma((10,)), dma((4,)), dma((6,)), dma((6,)), dma((15,)), dma((16,)),
            dma((1,)), dma((1,)), dma((3,)), dma((3,)), dma((12,)), dma((12,)),
            dma((6,)), dma((6,)), dma((4,)), dma((4,)), dma((3,)), dma((3,)),
        ],
        compiler_params=pltpu.CompilerParams(
            collective_id=0, has_side_effects=True, vmem_limit_bytes=58 * 1024 * 1024
        ),
        name="pyramid",
    )(
        features.reshape(PIXELS, CHANNELS),
        jnp.transpose(dilated_weight, (0, 1, 2, 4, 3)).reshape(TERMS - OWN, CHANNELS),
        point_weight.T,
        project_weight.reshape(4, MEMBERS, OWN, OUTPUTS),
        cotangent.reshape(PIXELS, OUTPUTS),
        branch_bias,
        project_bias.reshape(1, OUTPUTS),
    )
    return (jnp.transpose(head, (0, 2, 1)), grad.reshape(HEIGHT, BREADTH, BLOCK))


def solution(mesh):
    in_specs = (
        P("rows", None, None),
        P(None, "filt"),
        P(None, None, None, None, "filt"),
        P(None, "filt"),
        P(),
        P(),
        P("rows", None, None),
    )
    out_specs = (P("rows", None, "filt"), P("rows", None, "filt"))
    return jax.shard_map(
        on_device, mesh=mesh, in_specs=in_specs, out_specs=out_specs, check_vma=False
    )
```

time: 507 us -> 93.9 us (0.19)
  the two profiles are of different devices: /device:TPU:2 before, /device:TPU:33 now
where the time goes in v1:
time: 93.9 us; the launch traced here: 93.7 us
  Pallas kernels  90.1 us (96%)
  local copies, waits for them, and re-layouts  3 us (3%)
    pallas_call x1, Pallas kernels, on_device(): pl.pallas_call(kernel, out_shape=(jax.ShapeDtypeStruct((HEIGHT, OWN, BREA...  90.1 us
    unnamed x2, local copies, waits for them, and re-layouts  3 us

profile of v1, /device:TPU:33, one launch (start us, length us, event | category | flops | bytes accessed | tf_op | source)
XLA Modules:
  0.0 93.7 jit_solution(160391064403971971)
XLA Ops:
  0.6 90.1 %pyramid.1 = (bf16[12,16,48]{2,1,0:T(8,128)(2,1)}, bf16[576,128]{1,0:T(8,128)(2,1)}) custom-call(bf16[576,2048]{1,0:T(8,128)(2,1)} %bitcast.10, bf16[432,2048]{1,0:T(8,128)(2,1)} %bitcast.11, bf16[16,2048]{1,0:T(8,128)(2,1)} %bitcast.15, bf16[4,16,16,256]{3,2,1,0:T(8,128)(2,1)} %bitcast.12, bf16[576,256]{1,0:T(8,128)(2,1)} %bitcast.13, f32[4,16]{1,0:T(4,128)} %bias_hbm.1, ...), custom_call_target="tpu_custom_call" | custom-call | tf_op jit(solution)/shard_map/pyramid/pallas_call | solution.py:390
  90.7 1.4 %copy.11 = bf16[12,48,16]{1,2,0:T(8,128)(2,1)} copy(bf16[12,48,16]{1,2,0:T(8,128)(2,1)} %bitcast.16) | data formatting | bytes 36864
  92.1 1.6 %copy.12 = bf16[12,48,128]{2,1,0:T(8,128)(2,1)} copy(bf16[12,48,128]{2,1,0:T(8,128)(2,1)} %bitcast.14) | data formatting | bytes 294912

commit v2 on v1

v2 whole, which is shorter than its diff:
```python
import jax
import jax.numpy as jnp
from jax import lax
from jax.experimental import pallas as pl
from jax.experimental.pallas import tpu as pltpu
from jax.sharding import PartitionSpec as P

FIRST_DILATION = 12
SECOND_DILATION = 24
THIRD_DILATION = 36
DILATIONS = (FIRST_DILATION, SECOND_DILATION, THIRD_DILATION)
ROW_BLOCKS = 64
HEIGHT = 12
BREADTH = 48
PIXELS = HEIGHT * BREADTH
LANES = 640
CHANNELS = 2048
OWN = 16
TAPS = 28
TERMS = TAPS * OWN
MEMBERS = 16
OUTPUTS = 256
BLOCK = 128
PIECE_ROWS = TERMS // 4
PIECE_LANES = 256
MESH = pl.DeviceIdType.MESH
BF16 = jnp.bfloat16
F32 = jnp.float32


def device(x, y, z, core):
    x, y, z = lax.rem(x + 4, 4), lax.rem(y + 4, 4), lax.rem(z + 32, 32)
    return (lax.rem(z, 16) * 4 + x, (y * 2 + z // 16) * 2 + core)


def remote(source, target, send_sem, recv_sem, where):
    return pltpu.make_async_remote_copy(
        src_ref=source,
        dst_ref=target,
        send_sem=send_sem,
        recv_sem=recv_sem,
        device_id=where,
        device_id_type=MESH,
    )


def kernel(
    x_hbm, dilated_hbm, point_hbm, project_hbm, cot_hbm, bias_hbm, project_bias_hbm,
    head_ref, grad_ref,
    bias_ref, project_bias_ref, x_buf, w_buf, w_both, project, project_t, cot_buf, cot_t, columns,
    taps, row_send, row_recv, acts, pre, grads, grad_recv, spread, spread_t,
    part_sum, part_low, core_recv, sum_send, sum_recv,
    near, far, load_sem, fill_sem, row_ss, row_rs, act_ss, act_rs, first_ss, first_rs, zg_ss, zg_rs,
    xg_ss, xg_rs, grow_ss, grow_rs, core_ss, core_rs, sum_ss, sum_rs,
):
    row = lax.axis_index("rows")
    member = lax.axis_index("filt")
    x, z_low = lax.rem(row, 4), row // 4
    y, half, core = member // 4, lax.rem(member // 2, 2), lax.rem(member, 2)
    z = half * 16 + z_low
    z_quarter = lax.rem(z_low, 4)
    other = member + 2 - 4 * half
    twin = 1 - 2 * core

    def row_offset(slot):
        return (slot // 2 + 1) * (1 - 2 * (slot % 2))

    def sends(slot):
        place = row + row_offset(slot)
        return jnp.logical_and(place >= 0, place < ROW_BLOCKS)

    def gets(slot):
        place = row - row_offset(slot)
        return jnp.logical_and(place >= 0, place < ROW_BLOCKS)

    opposite = device(x, y, z + 16, core)
    eighth = device(x, y, z + jnp.where(z_low >= 8, 8, -8), core)
    partner = device(x, y, z, 1 - core)
    y_steps = (2, 1, 3)
    z_up, z_down = device(x, y, z + 4, core), device(x, y, z - 4, core)
    z_ahead = device(x, y, z + 8, core)

    def at_y(step, side):
        return (lax.rem(y + step, 4) * 2 + side) * 2 + core

    z_base = z - z_quarter
    z_peers = [device(x, y, z_base + lax.rem(z_quarter + d, 4), core) for d in (1, 2, 3)]
    x_peers = [device(x + d, y, z, core) for d in (1, 2, 3)]

    sent, due = [], {}

    def start(key, copy, gives=None, takes=None):
        sent.append((copy, gives))
        due[key] = (copy, takes)
        if gives is None:
            copy.start()
        else:
            pl.when(gives)(copy.start)

    def arrive(key):
        copy, takes = due.pop(key)
        if takes is None:
            copy.wait_recv()
        else:
            pl.when(takes)(copy.wait_recv)

    def finish():
        for key in list(due):
            arrive(key)
        for copy, gives in sent:
            if gives is None:
                copy.wait_send()
            else:
                pl.when(gives)(copy.wait_send)
        for load in list(loading):
            loaded(load)

    loading = {}

    def load(key, source, target, sem):
        loading[key] = pltpu.make_async_copy(source, target, sem)
        loading[key].start()

    def loaded(key):
        loading.pop(key).wait()

    halves = [pl.ds(n * (CHANNELS // 2), CHANNELS // 2) for n in range(2)]
    for n in range(2):
        load(
            ("x", n), x_hbm.at[:, halves[n]], x_buf.at[pl.ds(0, PIXELS), halves[n]], load_sem.at[n]
        )
        load(
            ("w", n),
            dilated_hbm.at[:, halves[n]],
            w_buf.at[pl.ds(0, TERMS - OWN), halves[n]],
            load_sem.at[2 + n],
        )
        load(
            ("p", n),
            point_hbm.at[:, halves[n]],
            w_buf.at[pl.ds(TERMS - OWN, OWN), halves[n]],
            load_sem.at[4 + n],
        )
    barrier = pltpu.get_barrier_semaphore()
    fixed_peers = (
        [partner, z_up, z_down] + z_peers + x_peers
        + [device(x, y + d, z, c) for d in y_steps for c in range(2)]
    )
    for peer in fixed_peers:
        pl.semaphore_signal(barrier, inc=1, device_id=peer, device_id_type=MESH)
    heard = jnp.int32(len(fixed_peers))
    for slot in range(6):
        @pl.when(sends(slot))
        def _():
            pl.semaphore_signal(
                barrier, inc=1, device_id=(row + row_offset(slot), member), device_id_type=MESH
            )
        heard = heard + sends(slot).astype(jnp.int32)

    load("bias", bias_hbm, bias_ref, load_sem.at[6])
    load("cot", cot_hbm, cot_buf.at[pl.ds(0, PIXELS)], load_sem.at[7])
    for k in range(4):
        load(("project", k), project_hbm.at[k], project.at[:, k], load_sem.at[8 + k])
    load("project_bias", project_bias_hbm, project_bias_ref, load_sem.at[12])
    x_buf[pl.ds(PIXELS, LANES - PIXELS), :] = jnp.zeros((LANES - PIXELS, CHANNELS), BF16)
    cot_buf[pl.ds(PIXELS, LANES - PIXELS), :] = jnp.zeros((LANES - PIXELS, OUTPUTS), BF16)
    for n in range(2):
        for key in ("x", "w", "p"):
            loaded((key, n))
        product = lax.dot_general(
            w_buf[:, halves[n]],
            x_buf[:, halves[n]],
            (((1,), (1,)), ((), ())),
            preferred_element_type=F32,
        )
        taps[...] = product if n == 0 else taps[...] + product
    for block in range(4):
        lanes = pl.multiple_of(block * 512 + half * 256, 256)
        load(
            ("fill", block),
            w_buf.at[:, pl.ds(lanes, 256)],
            w_both.at[pl.ds(0, TERMS), pl.ds(block * 256, 256)],
            fill_sem.at[block],
        )
    column = lax.rem(lax.broadcasted_iota(jnp.int32, (1, LANES), 1), BREADTH)

    def shift_columns(field, amount):
        if amount == 0:
            return field
        inside = jnp.logical_and(column + amount >= 0, column + amount < BREADTH)
        return jnp.where(inside, pltpu.roll(field, (-amount) % LANES, 1), 0.0)

    def tap(k, i, j):
        return taps[pl.ds((9 * k + 3 * i + j) * OWN, OWN), :]

    def row_sum(k, i):
        d = DILATIONS[k]
        return (
            shift_columns(tap(k, i, 0), -d) + tap(k, i, 1) + shift_columns(tap(k, i, 2), d)
        )

    for k in range(3):
        row_send[2 * k] = row_sum(k, 0)
        row_send[2 * k + 1] = row_sum(k, 2)
    pl.semaphore_wait(barrier, heard)
    for n, peer in ((0, z_up), (1, z_down)):
        pl.semaphore_signal(near.at[n], inc=1, device_id=peer, device_id_type=MESH)
    for slot in (4, 5, 2, 3, 0, 1):
        start(
            ("row", slot),
            remote(
                row_send.at[slot], row_recv.at[slot], row_ss.at[slot], row_rs.at[slot],
                (row + row_offset(slot), member),
            ),
            sends(slot),
            gets(slot),
        )

    z_rows = pl.multiple_of(z_quarter * PIECE_ROWS, 16)
    far_rows = pl.multiple_of(TERMS + z_quarter * PIECE_ROWS, 16)
    far_lanes = pl.multiple_of(x * PIECE_LANES, 128)
    give_lanes = pl.multiple_of(x * 512 + (1 - half) * 256, 256)
    for n in range(2):
        pl.semaphore_wait(near.at[n], 1)
    pl.semaphore_signal(far.at[0], inc=1, device_id=z_ahead, device_id_type=MESH)
    start(
        "first",
        remote(
            w_buf.at[pl.ds(z_rows, PIECE_ROWS), pl.ds(give_lanes, PIECE_LANES)],
            w_both.at[pl.ds(far_rows, PIECE_ROWS), pl.ds(far_lanes, PIECE_LANES)],
            first_ss.at[0], first_rs.at[0], eighth,
        ),
    )

    def diagonal(values, size):
        same = lax.broadcasted_iota(jnp.int32, (size, size), 0) == lax.broadcasted_iota(
            jnp.int32, (size, size), 1
        )
        return jnp.sum(
            jnp.where(same, jnp.broadcast_to(values, (size, size)), 0.0), axis=1, keepdims=True
        )

    loaded("bias")
    bias = bias_ref[...]
    biases = [diagonal(bias[k:k + 1, :], OWN) for k in range(4)]
    acts[member, pl.ds(0, OWN), :] = jnp.maximum(
        taps[pl.ds(TERMS - OWN, OWN), :] + biases[0], 0.0
    ).astype(BF16)
    centres = [row_sum(k, 1) + biases[k + 1] for k in range(3)]

    def send_acts(block, part, where, arriving):
        n = len(passed)
        passed.append(block)
        rows = pl.ds(0, 4 * OWN) if part is None else pl.ds(part * 2 * OWN, 2 * OWN)
        place = 0 if part is None else part

        def copy(of):
            ref = acts.at[of, rows]
            return remote(ref, ref, act_ss.at[n], act_rs.at[of, place], where)

        start(("act", n), copy(block))
        due[("act", n)] = (copy(arriving), None)
        return ("act", n)

    passed = []
    from_opposite = []
    for k in range(3):
        total = centres[k]
        for slot in (2 * k, 2 * k + 1):
            arrive(("row", slot))
            total = total + jnp.where(gets(slot), row_recv[slot], 0.0)
        acts[member, pl.ds((k + 1) * OWN, OWN), :] = jnp.maximum(total, 0.0).astype(BF16)
        if k == 0:
            pl.semaphore_wait(far.at[0], 1)
        if k in (0, 2):
            from_opposite.append(send_acts(member, k // 2, opposite, other))
    own_y = {}
    for d in y_steps:
        own_y[4 - d] = send_acts(
            member, None, device(x, y + d, z, core), at_y(4 - d, half)
        )
    rest = [send_acts(member, None, partner, member + twin)]

    for k in range(4):
        loaded(("project", k))
    loaded("cot")
    loaded("project_bias")
    project_t[...] = project[...].reshape(MEMBERS * 4 * OWN, OUTPUTS).T
    cot_t[...] = cot_buf[...].astype(F32).T
    columns[...] = jnp.broadcast_to(diagonal(project_bias_ref[...], OUTPUTS), (OUTPUTS, BLOCK))
    for d in (1, 3, 2):
        arrive(own_y[d])
        block = at_y(d, half)
        rest.append(send_acts(block, None, partner, block + twin))
    def far_piece(d):
        rows_from = pl.multiple_of(
            TERMS + lax.rem(z_quarter + 4 - d, 4) * PIECE_ROWS, 16
        )
        return w_both.at[pl.ds(rows_from, PIECE_ROWS), pl.ds(far_lanes, PIECE_LANES)]

    def spread_x(d):
        for e in (1, 2, 3):
            n = 3 * d + e - 1
            start(
                ("x", d, e),
                remote(far_piece(d), far_piece(d), xg_ss.at[n], xg_rs.at[n], x_peers[e - 1]),
            )

    arrive("first")
    for d in (1, 2, 3):
        start(
            ("z", d),
            remote(
                far_piece(0), far_piece(0), zg_ss.at[d - 1], zg_rs.at[d - 1], z_peers[d - 1]
            ),
        )
    spread_x(0)
    for part in range(2):
        arrive(from_opposite[part])
        for d in y_steps:
            for c in range(2):
                where = device(x, y + d, z, core + c * twin)
                rest.append(send_acts(other, part, where, at_y(4 - d, 1 - half) + c * twin))
        rest.append(send_acts(other, part, partner, other + twin))
        if part == 0:
            for d in (1, 2, 3):
                arrive(("z", d))
                spread_x(d)
    for key in rest:
        arrive(key)
    pre[...] = (
        jnp.dot(
            project_t[...],
            acts[...].reshape(MEMBERS * 4 * OWN, LANES),
            preferred_element_type=F32,
        )
        + columns[:, 0:1]
    )
    head_grad = jnp.where(pre[...] > 0, cot_t[...], 0.0).astype(BF16)
    for side, block in ((0, member), (1, other)):
        act_grad = jnp.dot(
            project[block].reshape(4 * OWN, OUTPUTS), head_grad, preferred_element_type=F32
        )
        branch_grad = jnp.where(acts[block] > 0, act_grad, 0.0).astype(BF16)
        for k in range(4):
            grads[k, pl.ds(side * OWN, OWN), :] = branch_grad[k * OWN:(k + 1) * OWN]
    for slot in (4, 5, 2, 3, 0, 1):
        start(
            ("grad", slot),
            remote(
                grads.at[slot // 2 + 1], grad_recv.at[slot], grow_ss.at[slot], grow_rs.at[slot],
                (row + row_offset(slot), member),
            ),
            sends(slot),
            gets(slot),
        )

    own_head = jnp.maximum(pre[pl.ds(pl.multiple_of(member * OWN, OWN), OWN), :], 0.0)
    for r in range(HEIGHT):
        head_ref[r] = own_head[:, r * BREADTH:(r + 1) * BREADTH].astype(BF16)

    def put(values, t):
        low = values.astype(BF16)
        for side in range(2):
            spread[pl.ds(side * TERMS + t * OWN, OWN), :] = low[side * OWN:(side + 1) * OWN]

    def put_columns(field, k, i):
        for j in range(3):
            put(shift_columns(field, -(j - 1) * DILATIONS[k]), 9 * k + 3 * i + j)

    put(grads[0].astype(F32), TAPS - 1)
    for k in range(3):
        put_columns(grads[k + 1].astype(F32), k, 1)
    for k in range(3):
        for slot, i in ((2 * k, 2), (2 * k + 1, 0)):
            arrive(("grad", slot))
            put_columns(jnp.where(gets(slot), grad_recv[slot].astype(F32), 0.0), k, i)
    spread_t[...] = spread[...].T

    for block in range(4):
        loaded(("fill", block))
    for d in range(4):
        for e in (1, 2, 3):
            arrive(("x", d, e))
    order = (2, 1, 3, 0)

    def multiply(n):
        lanes = pl.multiple_of(lax.rem(y + order[n], 4) * 256, 256)
        product = jnp.dot(
            spread_t[pl.ds(0, PIXELS), :], w_both[:, pl.ds(lanes, 256)], preferred_element_type=F32
        )
        for c in range(2):
            piece = product[:, c * BLOCK:(c + 1) * BLOCK]
            part_sum[n, c] = piece
            part_low[n, c] = piece.astype(BF16)
        start(
            ("core", n),
            remote(part_low.at[n, 1 - core], core_recv.at[n], core_ss.at[n], core_rs.at[n], partner),
        )

    def send_sum(n):
        arrive(("core", n))
        sum_send[n] = (part_sum[n, core] + core_recv[n].astype(F32)).astype(BF16)
        start(
            ("sum", n),
            remote(
                sum_send.at[n], sum_recv.at[n], sum_ss.at[n], sum_rs.at[n],
                device(x, y + order[n], z, core),
            ),
        )

    for n in range(3):
        multiply(n)
    send_sum(0)
    multiply(3)
    send_sum(1)
    send_sum(2)
    arrive(("core", 3))
    total = part_sum[3, core] + core_recv[3].astype(F32)
    for n in (1, 2, 0):
        arrive(("sum", n))
        total = total + sum_recv[n].astype(F32)
    grad_ref[...] = total.astype(BF16)
    finish()


def hand_out(head_in, grad_in, head_out, grad_out, sems):
    copies = [
        pltpu.make_async_copy(head_in, head_out, sems.at[0]),
        pltpu.make_async_copy(grad_in, grad_out, sems.at[1]),
    ]
    for copy in copies:
        copy.start()
    for copy in copies:
        copy.wait()


def on_device(
    features, point_weight, dilated_weight, branch_bias, project_weight, project_bias, cotangent
):
    in_place = pl.BlockSpec(memory_space=pltpu.HBM)
    vmem = pl.BlockSpec(memory_space=pltpu.VMEM)
    dma = pltpu.SemaphoreType.DMA
    head, grad = pl.pallas_call(
        kernel,
        out_shape=(
            jax.ShapeDtypeStruct((HEIGHT, OWN, BREADTH), BF16),
            jax.ShapeDtypeStruct((PIXELS, BLOCK), BF16),
        ),
        in_specs=[in_place] * 7,
        out_specs=(vmem, vmem),
        scratch_shapes=[
            pltpu.VMEM((4, OWN), F32),
            pltpu.VMEM((1, OUTPUTS), F32),
            pltpu.VMEM((LANES, CHANNELS), BF16),
            pltpu.VMEM((TERMS, CHANNELS), BF16),
            pltpu.VMEM((2 * TERMS, CHANNELS // 2), BF16),
            pltpu.VMEM((MEMBERS, 4, OWN, OUTPUTS), BF16),
            pltpu.VMEM((OUTPUTS, MEMBERS * 4 * OWN), BF16),
            pltpu.VMEM((LANES, OUTPUTS), BF16),
            pltpu.VMEM((OUTPUTS, LANES), F32),
            pltpu.VMEM((OUTPUTS, BLOCK), F32),
            pltpu.VMEM((TERMS, LANES), F32),
            pltpu.VMEM((6, OWN, LANES), F32),
            pltpu.VMEM((6, OWN, LANES), F32),
            pltpu.VMEM((MEMBERS, 4 * OWN, LANES), BF16),
            pltpu.VMEM((OUTPUTS, LANES), F32),
            pltpu.VMEM((4, 2 * OWN, LANES), BF16),
            pltpu.VMEM((6, 2 * OWN, LANES), BF16),
            pltpu.VMEM((2 * TERMS, LANES), BF16),
            pltpu.VMEM((LANES, 2 * TERMS), BF16),
            pltpu.VMEM((4, 2, PIXELS, BLOCK), F32),
            pltpu.VMEM((4, 2, PIXELS, BLOCK), BF16),
            pltpu.VMEM((4, PIXELS, BLOCK), BF16),
            pltpu.VMEM((3, PIXELS, BLOCK), BF16),
            pltpu.VMEM((3, PIXELS, BLOCK), BF16),
            pltpu.SemaphoreType.REGULAR((2,)), pltpu.SemaphoreType.REGULAR((1,)),
            dma((13,)), dma((4,)), dma((6,)), dma((6,)), dma((23,)), dma((16, 2)),
            dma((1,)), dma((1,)), dma((3,)), dma((3,)), dma((12,)), dma((12,)),
            dma((6,)), dma((6,)), dma((4,)), dma((4,)), dma((3,)), dma((3,)),
        ],
        compiler_params=pltpu.CompilerParams(
            collective_id=0, has_side_effects=True, vmem_limit_bytes=58 * 1024 * 1024
        ),
        name="pyramid",
    )(
        features.reshape(PIXELS, CHANNELS),
        jnp.transpose(dilated_weight, (0, 1, 2, 4, 3)).reshape(TERMS - OWN, CHANNELS),
        point_weight.T,
        project_weight.reshape(4, MEMBERS, OWN, OUTPUTS),
        cotangent.reshape(PIXELS, OUTPUTS),
        branch_bias,
        project_bias.reshape(1, OUTPUTS),
    )
    head, grad = pl.pallas_call(
        hand_out,
        out_shape=(
            jax.ShapeDtypeStruct((HEIGHT, OWN, BREADTH), BF16),
            jax.ShapeDtypeStruct((PIXELS, BLOCK), BF16),
        ),
        in_specs=[vmem] * 2,
        out_specs=(in_place, in_place),
        scratch_shapes=[dma((2,))],
        name="hand_out",
    )(head, grad)
    return (jnp.transpose(head, (0, 2, 1)), grad.reshape(HEIGHT, BREADTH, BLOCK))


def solution(mesh):
    in_specs = (
        P("rows", None, None),
        P(None, "filt"),
        P(None, None, None, None, "filt"),
        P(None, "filt"),
        P(),
        P(),
        P("rows", None, None),
    )
    out_specs = (P("rows", None, "filt"), P("rows", None, "filt"))
    return jax.shard_map(
        on_device, mesh=mesh, in_specs=in_specs, out_specs=out_specs, check_vma=False
    )
```

time: 93.9 us -> 89.3 us (0.951)
  local copies, waits for them, and re-layouts: 3 us -> 0 us
  Pallas kernels: 90.1 us -> 88.5 us
    pallas_call x1, Pallas kernels: 90.1 us -> 86.9 us  [on_device(): pl.pallas_call(kernel, out_shape=(jax.ShapeDtypeStruct((HEIGHT, OWN, BREA...]
    unnamed x2 -> x0, local copies, waits for them, and re-layouts: 3 us -> none
    pallas_call x0 -> x1, Pallas kernels: none -> 1.63 us  [on_device(): pl.pallas_call(hand_out, out_shape=(jax.ShapeDtypeStruct((HEIGHT, OWN, BR...]
where the time goes in v2:
time: 89.3 us; the launch traced here: 89.1 us
  Pallas kernels  88.5 us (99%)
    pallas_call x1, Pallas kernels, on_device(): pl.pallas_call(kernel, out_shape=(jax.ShapeDtypeStruct((HEIGHT, OWN, BREA...  86.9 us

profile of v2, /device:TPU:33, one launch (start us, length us, event | category | flops | bytes accessed | tf_op | source)
XLA Modules:
  0.0 89.1 jit_solution(346044998284841330)
XLA Ops:
  0.6 86.9 %pyramid.1 = (bf16[12,16,48]{2,1,0:T(8,128)(2,1)}, bf16[576,128]{1,0:T(8,128)(2,1)}) custom-call(bf16[576,2048]{1,0:T(8,128)(2,1)} %bitcast.10, bf16[432,2048]{1,0:T(8,128)(2,1)} %bitcast.11, bf16[16,2048]{1,0:T(8,128)(2,1)} %bitcast.14, bf16[4,16,16,256]{3,2,1,0:T(8,128)(2,1)} %bitcast.12, bf16[576,256]{1,0:T(8,128)(2,1)} %bitcast.13, f32[4,16]{1,0:T(4,128)} %bias_hbm.1, ...), custom_call_target="tpu_custom_call" | custom-call | tf_op jit(solution)/shard_map/pyramid/pallas_call | solution.py:444
  87.5 1.6 %hand_out.1 = (bf16[12,16,48]{2,1,0:T(8,128)(2,1)}, bf16[576,128]{1,0:T(8,128)(2,1)}) custom-call(bf16[12,16,48]{2,1,0:T(8,128)(2,1)} %get-tuple-element.6.head_in, bf16[576,128]{1,0:T(8,128)(2,1)} %get-tuple-element.7.grad_in), custom_call_target="tpu_custom_call" | custom-call | tf_op jit(solution)/shard_map/hand_out/pallas_call | solution.py:495

commit v3 on v2

--- a/solution.py
+++ b/solution.py
@@ -50,7 +50,7 @@
     bias_ref, project_bias_ref, x_buf, w_buf, w_both, project, project_t, cot_buf, cot_t, columns,
     taps, row_send, row_recv, acts, pre, grads, grad_recv, spread, spread_t,
     part_sum, part_low, core_recv, sum_send, sum_recv,
-    near, far, load_sem, fill_sem, row_ss, row_rs, act_ss, act_rs, first_ss, first_rs, zg_ss, zg_rs,
+    far, load_sem, fill_sem, row_ss, row_rs, act_ss, act_rs, first_ss, first_rs, zg_ss, zg_rs,
     xg_ss, xg_rs, grow_ss, grow_rs, core_ss, core_rs, sum_ss, sum_rs,
 ):
     row = lax.axis_index("rows")
@@ -77,8 +77,7 @@
     eighth = device(x, y, z + jnp.where(z_low >= 8, 8, -8), core)
     partner = device(x, y, z, 1 - core)
     y_steps = (2, 1, 3)
-    z_up, z_down = device(x, y, z + 4, core), device(x, y, z - 4, core)
-    z_ahead = device(x, y, z + 8, core)
+    z_ahead, z_behind = device(x, y, z + 8, core), device(x, y, z - 8, core)
 
     def at_y(step, side):
         return (lax.rem(y + step, 4) * 2 + side) * 2 + core
@@ -104,14 +103,18 @@
         else:
             pl.when(takes)(copy.wait_recv)
 
-    def finish():
-        for key in list(due):
-            arrive(key)
+    def drain():
         for copy, gives in sent:
             if gives is None:
                 copy.wait_send()
             else:
                 pl.when(gives)(copy.wait_send)
+        sent.clear()
+
+    def finish():
+        for key in list(due):
+            arrive(key)
+        drain()
         for load in list(loading):
             loaded(load)
 
@@ -143,7 +146,7 @@
         )
     barrier = pltpu.get_barrier_semaphore()
     fixed_peers = (
-        [partner, z_up, z_down] + z_peers + x_peers
+        [partner, z_ahead, z_behind] + z_peers + x_peers
         + [device(x, y + d, z, c) for d in y_steps for c in range(2)]
     )
     for peer in fixed_peers:
@@ -174,13 +177,14 @@
             preferred_element_type=F32,
         )
         taps[...] = product if n == 0 else taps[...] + product
-    for block in range(4):
-        lanes = pl.multiple_of(block * 512 + half * 256, 256)
+    order = (2, 1, 3, 0)
+    for n in range(4):
+        lanes = pl.multiple_of(lax.rem(y + order[n], 4) * 512 + half * 256, 256)
         load(
-            ("fill", block),
+            ("fill", n),
             w_buf.at[:, pl.ds(lanes, 256)],
-            w_both.at[pl.ds(0, TERMS), pl.ds(block * 256, 256)],
-            fill_sem.at[block],
+            w_both.at[pl.ds(0, TERMS), pl.ds(n * 256, 256)],
+            fill_sem.at[n],
         )
     column = lax.rem(lax.broadcasted_iota(jnp.int32, (1, LANES), 1), BREADTH)
 
@@ -203,8 +207,7 @@
         row_send[2 * k] = row_sum(k, 0)
         row_send[2 * k + 1] = row_sum(k, 2)
     pl.semaphore_wait(barrier, heard)
-    for n, peer in ((0, z_up), (1, z_down)):
-        pl.semaphore_signal(near.at[n], inc=1, device_id=peer, device_id_type=MESH)
+    pl.semaphore_signal(far.at[0], inc=1, device_id=z_ahead, device_id_type=MESH)
     for slot in (4, 5, 2, 3, 0, 1):
         start(
             ("row", slot),
@@ -219,10 +222,8 @@
     z_rows = pl.multiple_of(z_quarter * PIECE_ROWS, 16)
     far_rows = pl.multiple_of(TERMS + z_quarter * PIECE_ROWS, 16)
     far_lanes = pl.multiple_of(x * PIECE_LANES, 128)
-    give_lanes = pl.multiple_of(x * 512 + (1 - half) * 256, 256)
-    for n in range(2):
-        pl.semaphore_wait(near.at[n], 1)
-    pl.semaphore_signal(far.at[0], inc=1, device_id=z_ahead, device_id_type=MESH)
+    ahead = jnp.where(x == 0, 2, jnp.where(x == 1, 1, jnp.where(x == 2, 3, 0)))
+    give_lanes = pl.multiple_of(lax.rem(y + ahead, 4) * 512 + (1 - half) * 256, 256)
     start(
         "first",
         remote(
@@ -251,7 +252,7 @@
     def send_acts(block, part, where, arriving):
         n = len(passed)
         passed.append(block)
-        rows = pl.ds(0, 4 * OWN) if part is None else pl.ds(part * 2 * OWN, 2 * OWN)
+        rows = pl.ds(0, 4 * OWN) if part is None else pl.ds(part * OWN, OWN)
         place = 0 if part is None else part
 
         def copy(of):
@@ -272,8 +273,8 @@
         acts[member, pl.ds((k + 1) * OWN, OWN), :] = jnp.maximum(total, 0.0).astype(BF16)
         if k == 0:
             pl.semaphore_wait(far.at[0], 1)
-        if k in (0, 2):
-            from_opposite.append(send_acts(member, k // 2, opposite, other))
+            from_opposite.append(send_acts(member, 0, opposite, other))
+        from_opposite.append(send_acts(member, k + 1, opposite, other))
     own_y = {}
     for d in y_steps:
         own_y[4 - d] = send_acts(
@@ -315,7 +316,7 @@
             ),
         )
     spread_x(0)
-    for part in range(2):
+    for part in range(4):
         arrive(from_opposite[part])
         for d in y_steps:
             for c in range(2):
@@ -337,24 +338,25 @@
         + columns[:, 0:1]
     )
     head_grad = jnp.where(pre[...] > 0, cot_t[...], 0.0).astype(BF16)
-    for side, block in ((0, member), (1, other)):
+    branch_grads = []
+    for block in (member, other):
         act_grad = jnp.dot(
             project[block].reshape(4 * OWN, OUTPUTS), head_grad, preferred_element_type=F32
         )
-        branch_grad = jnp.where(acts[block] > 0, act_grad, 0.0).astype(BF16)
-        for k in range(4):
-            grads[k, pl.ds(side * OWN, OWN), :] = branch_grad[k * OWN:(k + 1) * OWN]
-    for slot in (4, 5, 2, 3, 0, 1):
-        start(
-            ("grad", slot),
-            remote(
-                grads.at[slot // 2 + 1], grad_recv.at[slot], grow_ss.at[slot], grow_rs.at[slot],
-                (row + row_offset(slot), member),
-            ),
-            sends(slot),
-            gets(slot),
-        )
-
+        branch_grads.append(jnp.where(acts[block] > 0, act_grad, 0.0).astype(BF16))
+    for k in (3, 2, 1, 0):
+        for side in range(2):
+            grads[k, pl.ds(side * OWN, OWN), :] = branch_grads[side][k * OWN:(k + 1) * OWN]
+        for slot in (2 * k - 2, 2 * k - 1) if k else ():
+            start(
+                ("grad", slot),
+                remote(
+                    grads.at[k], grad_recv.at[slot], grow_ss.at[slot], grow_rs.at[slot],
+                    (row + row_offset(slot), member),
+                ),
+                sends(slot),
+                gets(slot),
+            )
     own_head = jnp.maximum(pre[pl.ds(pl.multiple_of(member * OWN, OWN), OWN), :], 0.0)
     for r in range(HEIGHT):
         head_ref[r] = own_head[:, r * BREADTH:(r + 1) * BREADTH].astype(BF16)
@@ -382,21 +384,25 @@
     for d in range(4):
         for e in (1, 2, 3):
             arrive(("x", d, e))
-    order = (2, 1, 3, 0)
-
-    def multiply(n):
-        lanes = pl.multiple_of(lax.rem(y + order[n], 4) * 256, 256)
+    def multiply(pair):
         product = jnp.dot(
-            spread_t[pl.ds(0, PIXELS), :], w_both[:, pl.ds(lanes, 256)], preferred_element_type=F32
-        )
-        for c in range(2):
-            piece = product[:, c * BLOCK:(c + 1) * BLOCK]
-            part_sum[n, c] = piece
-            part_low[n, c] = piece.astype(BF16)
-        start(
-            ("core", n),
-            remote(part_low.at[n, 1 - core], core_recv.at[n], core_ss.at[n], core_rs.at[n], partner),
-        )
+            spread_t[pl.ds(0, PIXELS), :],
+            w_both[:, pl.ds(pair * 512, 512)],
+            preferred_element_type=F32,
+        )
+        for n in (2 * pair, 2 * pair + 1):
+            for c in range(2):
+                lane = (n % 2) * 256 + c * BLOCK
+                piece = product[:, lane:lane + BLOCK]
+                part_sum[n, c] = piece
+                part_low[n, c] = piece.astype(BF16)
+            start(
+                ("core", n),
+                remote(
+                    part_low.at[n, 1 - core], core_recv.at[n], core_ss.at[n], core_rs.at[n],
+                    partner,
+                ),
+            )
 
     def send_sum(n):
         arrive(("core", n))
@@ -409,12 +415,11 @@
             ),
         )
 
+    multiply(0)
+    multiply(1)
     for n in range(3):
-        multiply(n)
-    send_sum(0)
-    multiply(3)
-    send_sum(1)
-    send_sum(2)
+        send_sum(n)
+    drain()
     arrive(("core", 3))
     total = part_sum[3, core] + core_recv[3].astype(F32)
     for n in (1, 2, 0):
@@ -444,8 +449,8 @@
     head, grad = pl.pallas_call(
         kernel,
         out_shape=(
-            jax.ShapeDtypeStruct((HEIGHT, OWN, BREADTH), BF16),
-            jax.ShapeDtypeStruct((PIXELS, BLOCK), BF16),
+            pltpu.VMEM((HEIGHT, OWN, BREADTH), BF16),
+            pltpu.VMEM((PIXELS, BLOCK), BF16),
         ),
         in_specs=[in_place] * 7,
         out_specs=(vmem, vmem),
@@ -474,8 +479,8 @@
             pltpu.VMEM((4, PIXELS, BLOCK), BF16),
             pltpu.VMEM((3, PIXELS, BLOCK), BF16),
             pltpu.VMEM((3, PIXELS, BLOCK), BF16),
-            pltpu.SemaphoreType.REGULAR((2,)), pltpu.SemaphoreType.REGULAR((1,)),
-            dma((13,)), dma((4,)), dma((6,)), dma((6,)), dma((23,)), dma((16, 2)),
+            pltpu.SemaphoreType.REGULAR((1,)),
+            dma((13,)), dma((4,)), dma((6,)), dma((6,)), dma((39,)), dma((16, 4)),
             dma((1,)), dma((1,)), dma((3,)), dma((3,)), dma((12,)), dma((12,)),
             dma((6,)), dma((6,)), dma((4,)), dma((4,)), dma((3,)), dma((3,)),
         ],
@@ -502,7 +507,7 @@
         out_specs=(in_place, in_place),
         scratch_shapes=[dma((2,))],
         name="hand_out",
-    )(head, grad)
+    )(*[pltpu.with_memory_space_constraint(value, pltpu.VMEM) for value in (head, grad)])
     return (jnp.transpose(head, (0, 2, 1)), grad.reshape(HEIGHT, BREADTH, BLOCK))
 
 

time: 89.3 us -> 87.8 us (0.983)
  Pallas kernels: 88.5 us -> 87 us
    pallas_call x1, Pallas kernels: 1.63 us -> 0.7 us  [on_device(): pl.pallas_call(hand_out, out_shape=(jax.ShapeDtypeStruct((HEIGHT, OWN, BR...]
where the time goes in v3:
time: 87.8 us; the launch traced here: 87.7 us
  Pallas kernels  87 us (99%)
    pallas_call x1, Pallas kernels, on_device(): pl.pallas_call(kernel, out_shape=(pltpu.VMEM((HEIGHT, OWN, BREADTH), BF16...  86.3 us

profile of v3, /device:TPU:33, one launch (start us, length us, event | category | flops | bytes accessed | tf_op | source)
XLA Modules:
  0.0 87.7 jit_solution(14266720620172069516)
XLA Ops:
  0.6 86.3 %pyramid.1 = (bf16[12,16,48]{2,1,0:T(8,128)(2,1)S(1)}, bf16[576,128]{1,0:T(8,128)(2,1)S(1)}) custom-call(bf16[576,2048]{1,0:T(8,128)(2,1)} %bitcast.10, bf16[432,2048]{1,0:T(8,128)(2,1)} %bitcast.11, bf16[16,2048]{1,0:T(8,128)(2,1)} %bitcast.14, bf16[4,16,16,256]{3,2,1,0:T(8,128)(2,1)} %bitcast.12, bf16[576,256]{1,0:T(8,128)(2,1)} %bitcast.13, ...), custom_call_target="tpu_custom_call" | custom-call | tf_op jit(solution)/shard_map/pyramid/pallas_call | solution.py:449
  87.0 0.7 hand_out.1

commit v4 on v3

--- a/solution.py
+++ b/solution.py
@@ -252,7 +252,7 @@
     def send_acts(block, part, where, arriving):
         n = len(passed)
         passed.append(block)
-        rows = pl.ds(0, 4 * OWN) if part is None else pl.ds(part * OWN, OWN)
+        rows = pl.ds(0, 4 * OWN) if part is None else pl.ds(part * 2 * OWN, 2 * OWN)
         place = 0 if part is None else part
 
         def copy(of):
@@ -273,8 +273,8 @@
         acts[member, pl.ds((k + 1) * OWN, OWN), :] = jnp.maximum(total, 0.0).astype(BF16)
         if k == 0:
             pl.semaphore_wait(far.at[0], 1)
-            from_opposite.append(send_acts(member, 0, opposite, other))
-        from_opposite.append(send_acts(member, k + 1, opposite, other))
+        if k in (0, 2):
+            from_opposite.append(send_acts(member, k // 2, opposite, other))
     own_y = {}
     for d in y_steps:
         own_y[4 - d] = send_acts(
@@ -308,15 +308,8 @@
             )
 
     arrive("first")
-    for d in (1, 2, 3):
-        start(
-            ("z", d),
-            remote(
-                far_piece(0), far_piece(0), zg_ss.at[d - 1], zg_rs.at[d - 1], z_peers[d - 1]
-            ),
-        )
     spread_x(0)
-    for part in range(4):
+    for part in range(2):
         arrive(from_opposite[part])
         for d in y_steps:
             for c in range(2):
@@ -325,8 +318,15 @@
         rest.append(send_acts(other, part, partner, other + twin))
         if part == 0:
             for d in (1, 2, 3):
-                arrive(("z", d))
-                spread_x(d)
+                start(
+                    ("z", d),
+                    remote(
+                        far_piece(0), far_piece(0), zg_ss.at[d - 1], zg_rs.at[d - 1], z_peers[d - 1]
+                    ),
+                )
+    for d in (1, 2, 3):
+        arrive(("z", d))
+        spread_x(d)
     for key in rest:
         arrive(key)
     pre[...] = (
@@ -480,7 +480,7 @@
             pltpu.VMEM((3, PIXELS, BLOCK), BF16),
             pltpu.VMEM((3, PIXELS, BLOCK), BF16),
             pltpu.SemaphoreType.REGULAR((1,)),
-            dma((13,)), dma((4,)), dma((6,)), dma((6,)), dma((39,)), dma((16, 4)),
+            dma((13,)), dma((4,)), dma((6,)), dma((6,)), dma((23,)), dma((16, 2)),
             dma((1,)), dma((1,)), dma((3,)), dma((3,)), dma((12,)), dma((12,)),
             dma((6,)), dma((6,)), dma((4,)), dma((4,)), dma((3,)), dma((3,)),
         ],

time: 87.8 us -> 89.1 us (1.015)
  Pallas kernels: 87 us -> 88.3 us
    pallas_call x1, Pallas kernels: 86.3 us -> 87.6 us  [on_device(): pl.pallas_call(kernel, out_shape=(pltpu.VMEM((HEIGHT, OWN, BREADTH), BF16...]
where the time goes in v4:
time: 89.1 us; the launch traced here: 89 us
  Pallas kernels  88.3 us (99%)
    pallas_call x1, Pallas kernels, on_device(): pl.pallas_call(kernel, out_shape=(pltpu.VMEM((HEIGHT, OWN, BREADTH), BF16...  87.6 us

profile of v4, /device:TPU:33, one launch (start us, length us, event | category | flops | bytes accessed | tf_op | source)
XLA Modules:
  0.0 89.0 jit_solution(9873685933607239926)
XLA Ops:
  0.6 87.6 %pyramid.1 = (bf16[12,16,48]{2,1,0:T(8,128)(2,1)S(1)}, bf16[576,128]{1,0:T(8,128)(2,1)S(1)}) custom-call(bf16[576,2048]{1,0:T(8,128)(2,1)} %bitcast.10, bf16[432,2048]{1,0:T(8,128)(2,1)} %bitcast.11, bf16[16,2048]{1,0:T(8,128)(2,1)} %bitcast.14, bf16[4,16,16,256]{3,2,1,0:T(8,128)(2,1)} %bitcast.12, bf16[576,256]{1,0:T(8,128)(2,1)} %bitcast.13, ...), custom_call_target="tpu_custom_call" | custom-call | tf_op jit(solution)/shard_map/pyramid/pallas_call | solution.py:449
  88.3 0.7 hand_out.1

commit v5 on v4

--- a/solution.py
+++ b/solution.py
@@ -74,7 +74,11 @@
         return jnp.logical_and(place >= 0, place < ROW_BLOCKS)
 
     opposite = device(x, y, z + 16, core)
-    eighth = device(x, y, z + jnp.where(z_low >= 8, 8, -8), core)
+    group = z_low // 4
+    outer = jnp.logical_or(group == 0, group == 3)
+    inner = jnp.logical_not(outer)
+    inward = jnp.where(group < 2, 4, -4)
+    z_outward, z_inward = device(x, y, z - inward, core), device(x, y, z + inward, core)
     partner = device(x, y, z, 1 - core)
     y_steps = (2, 1, 3)
     z_ahead, z_behind = device(x, y, z + 8, core), device(x, y, z - 8, core)
@@ -127,26 +131,9 @@
     def loaded(key):
         loading.pop(key).wait()
 
-    halves = [pl.ds(n * (CHANNELS // 2), CHANNELS // 2) for n in range(2)]
-    for n in range(2):
-        load(
-            ("x", n), x_hbm.at[:, halves[n]], x_buf.at[pl.ds(0, PIXELS), halves[n]], load_sem.at[n]
-        )
-        load(
-            ("w", n),
-            dilated_hbm.at[:, halves[n]],
-            w_buf.at[pl.ds(0, TERMS - OWN), halves[n]],
-            load_sem.at[2 + n],
-        )
-        load(
-            ("p", n),
-            point_hbm.at[:, halves[n]],
-            w_buf.at[pl.ds(TERMS - OWN, OWN), halves[n]],
-            load_sem.at[4 + n],
-        )
     barrier = pltpu.get_barrier_semaphore()
     fixed_peers = (
-        [partner, z_ahead, z_behind] + z_peers + x_peers
+        [z_ahead, z_behind, z_outward, z_inward, partner] + z_peers + x_peers
         + [device(x, y + d, z, c) for d in y_steps for c in range(2)]
     )
     for peer in fixed_peers:
@@ -160,6 +147,23 @@
             )
         heard = heard + sends(slot).astype(jnp.int32)
 
+    halves = [pl.ds(n * (CHANNELS // 2), CHANNELS // 2) for n in range(2)]
+    for n in range(2):
+        load(
+            ("x", n), x_hbm.at[:, halves[n]], x_buf.at[pl.ds(0, PIXELS), halves[n]], load_sem.at[n]
+        )
+        load(
+            ("w", n),
+            dilated_hbm.at[:, halves[n]],
+            w_buf.at[pl.ds(0, TERMS - OWN), halves[n]],
+            load_sem.at[2 + n],
+        )
+        load(
+            ("p", n),
+            point_hbm.at[:, halves[n]],
+            w_buf.at[pl.ds(TERMS - OWN, OWN), halves[n]],
+            load_sem.at[4 + n],
+        )
     load("bias", bias_hbm, bias_ref, load_sem.at[6])
     load("cot", cot_hbm, cot_buf.at[pl.ds(0, PIXELS)], load_sem.at[7])
     for k in range(4):
@@ -225,12 +229,14 @@
     ahead = jnp.where(x == 0, 2, jnp.where(x == 1, 1, jnp.where(x == 2, 3, 0)))
     give_lanes = pl.multiple_of(lax.rem(y + ahead, 4) * 512 + (1 - half) * 256, 256)
     start(
-        "first",
+        "give",
         remote(
             w_buf.at[pl.ds(z_rows, PIECE_ROWS), pl.ds(give_lanes, PIECE_LANES)],
             w_both.at[pl.ds(far_rows, PIECE_ROWS), pl.ds(far_lanes, PIECE_LANES)],
-            first_ss.at[0], first_rs.at[0], eighth,
+            first_ss.at[0], first_rs.at[0], z_outward,
         ),
+        outer,
+        outer,
     )
 
     def diagonal(values, size):
@@ -249,6 +255,41 @@
     ).astype(BF16)
     centres = [row_sum(k, 1) + biases[k + 1] for k in range(3)]
 
+    def far_piece(d):
+        rows_from = pl.multiple_of(
+            TERMS + lax.rem(z_quarter + 4 - d, 4) * PIECE_ROWS, 16
+        )
+        return w_both.at[pl.ds(rows_from, PIECE_ROWS), pl.ds(far_lanes, PIECE_LANES)]
+
+    def spread_x(d, where):
+        for e in (1, 2, 3):
+            n = 3 * d + e - 1
+            start(
+                ("x", where is outer, d, e),
+                remote(far_piece(d), far_piece(d), xg_ss.at[n], xg_rs.at[n], x_peers[e - 1]),
+                where,
+                where,
+            )
+
+    def spread_z(where):
+        for d in (1, 2, 3):
+            start(
+                ("z", where is outer, d),
+                remote(
+                    far_piece(0), far_piece(0), zg_ss.at[d - 1], zg_rs.at[d - 1], z_peers[d - 1]
+                ),
+                where,
+                where,
+            )
+
+    def pass_z(where):
+        for d in (1, 2, 3):
+            arrive(("z", where is outer, d))
+            spread_x(d, where)
+
+    arrive("give")
+    spread_x(0, outer)
+
     def send_acts(block, part, where, arriving):
         n = len(passed)
         passed.append(block)
@@ -264,17 +305,14 @@
         return ("act", n)
 
     passed = []
-    from_opposite = []
     for k in range(3):
         total = centres[k]
         for slot in (2 * k, 2 * k + 1):
             arrive(("row", slot))
             total = total + jnp.where(gets(slot), row_recv[slot], 0.0)
         acts[member, pl.ds((k + 1) * OWN, OWN), :] = jnp.maximum(total, 0.0).astype(BF16)
-        if k == 0:
-            pl.semaphore_wait(far.at[0], 1)
-        if k in (0, 2):
-            from_opposite.append(send_acts(member, k // 2, opposite, other))
+    pl.semaphore_wait(far.at[0], 1)
+    from_opposite = [send_acts(member, part, opposite, other) for part in range(2)]
     own_y = {}
     for d in y_steps:
         own_y[4 - d] = send_acts(
@@ -293,22 +331,6 @@
         arrive(own_y[d])
         block = at_y(d, half)
         rest.append(send_acts(block, None, partner, block + twin))
-    def far_piece(d):
-        rows_from = pl.multiple_of(
-            TERMS + lax.rem(z_quarter + 4 - d, 4) * PIECE_ROWS, 16
-        )
-        return w_both.at[pl.ds(rows_from, PIECE_ROWS), pl.ds(far_lanes, PIECE_LANES)]
-
-    def spread_x(d):
-        for e in (1, 2, 3):
-            n = 3 * d + e - 1
-            start(
-                ("x", d, e),
-                remote(far_piece(d), far_piece(d), xg_ss.at[n], xg_rs.at[n], x_peers[e - 1]),
-            )
-
-    arrive("first")
-    spread_x(0)
     for part in range(2):
         arrive(from_opposite[part])
         for d in y_steps:
@@ -317,16 +339,17 @@
                 rest.append(send_acts(other, part, where, at_y(4 - d, 1 - half) + c * twin))
         rest.append(send_acts(other, part, partner, other + twin))
         if part == 0:
-            for d in (1, 2, 3):
-                start(
-                    ("z", d),
-                    remote(
-                        far_piece(0), far_piece(0), zg_ss.at[d - 1], zg_rs.at[d - 1], z_peers[d - 1]
-                    ),
-                )
-    for d in (1, 2, 3):
-        arrive(("z", d))
-        spread_x(d)
+            start(
+                "relay",
+                remote(far_piece(0), far_piece(0), first_ss.at[1], first_rs.at[1], z_inward),
+                outer,
+                inner,
+            )
+            spread_z(outer)
+    arrive("relay")
+    spread_z(inner)
+    spread_x(0, inner)
+    pass_z(outer)
     for key in rest:
         arrive(key)
     pre[...] = (
@@ -357,6 +380,8 @@
                 sends(slot),
                 gets(slot),
             )
+    pass_z(inner)
+
     own_head = jnp.maximum(pre[pl.ds(pl.multiple_of(member * OWN, OWN), OWN), :], 0.0)
     for r in range(HEIGHT):
         head_ref[r] = own_head[:, r * BREADTH:(r + 1) * BREADTH].astype(BF16)
@@ -383,7 +408,8 @@
         loaded(("fill", block))
     for d in range(4):
         for e in (1, 2, 3):
-            arrive(("x", d, e))
+            arrive(("x", True, d, e))
+            arrive(("x", False, d, e))
     def multiply(pair):
         product = jnp.dot(
             spread_t[pl.ds(0, PIXELS), :],
@@ -481,7 +507,7 @@
             pltpu.VMEM((3, PIXELS, BLOCK), BF16),
             pltpu.SemaphoreType.REGULAR((1,)),
             dma((13,)), dma((4,)), dma((6,)), dma((6,)), dma((23,)), dma((16, 2)),
-            dma((1,)), dma((1,)), dma((3,)), dma((3,)), dma((12,)), dma((12,)),
+            dma((2,)), dma((2,)), dma((3,)), dma((3,)), dma((12,)), dma((12,)),
             dma((6,)), dma((6,)), dma((4,)), dma((4,)), dma((3,)), dma((3,)),
         ],
         compiler_params=pltpu.CompilerParams(

time: 89.1 us -> 86.5 us (0.971)
  the two profiles are of different devices: /device:TPU:33 before, /device:TPU:67 now
where the time goes in v5:
time: 86.5 us; the launch traced here: 86.4 us
  Pallas kernels  85.7 us (99%)
    pallas_call x1, Pallas kernels, on_device(): pl.pallas_call(kernel, out_shape=(pltpu.VMEM((HEIGHT, OWN, BREADTH), BF16...  85 us

profile of v5, /device:TPU:67, one launch (start us, length us, event | category | flops | bytes accessed | tf_op | source)
XLA Modules:
  0.0 86.4 jit_solution(9888054299136383671)
XLA Ops:
  0.6 85.0 %pyramid.1 = (bf16[12,16,48]{2,1,0:T(8,128)(2,1)S(1)}, bf16[576,128]{1,0:T(8,128)(2,1)S(1)}) custom-call(bf16[576,2048]{1,0:T(8,128)(2,1)} %bitcast.10, bf16[432,2048]{1,0:T(8,128)(2,1)} %bitcast.11, bf16[16,2048]{1,0:T(8,128)(2,1)} %bitcast.14, bf16[4,16,16,256]{3,2,1,0:T(8,128)(2,1)} %bitcast.12, bf16[576,256]{1,0:T(8,128)(2,1)} %bitcast.13, ...), custom_call_target="tpu_custom_call" | custom-call | tf_op jit(solution)/shard_map/pyramid/pallas_call | solution.py:475
  85.7 0.7 hand_out.1

commit v6 on v5

--- a/solution.py
+++ b/solution.py
@@ -352,6 +352,7 @@
     pass_z(outer)
     for key in rest:
         arrive(key)
+    pass_z(inner)
     pre[...] = (
         jnp.dot(
             project_t[...],
@@ -380,7 +381,6 @@
                 sends(slot),
                 gets(slot),
             )
-    pass_z(inner)
 
     own_head = jnp.maximum(pre[pl.ds(pl.multiple_of(member * OWN, OWN), OWN), :], 0.0)
     for r in range(HEIGHT):

time: 86.5 us -> 86.5 us (level)
  no operation moved by 1% of the time
where the time goes in v6:
time: 86.5 us; the launch traced here: 86.4 us
  Pallas kernels  85.7 us (99%)
    pallas_call x1, Pallas kernels, on_device(): pl.pallas_call(kernel, out_shape=(pltpu.VMEM((HEIGHT, OWN, BREADTH), BF16...  85 us

profile of v6, /device:TPU:67, one launch (start us, length us, event | category | flops | bytes accessed | tf_op | source)
XLA Modules:
  0.0 86.4 jit_solution(7106828184106691745)
XLA Ops:
  0.6 85.0 %pyramid.1 = (bf16[12,16,48]{2,1,0:T(8,128)(2,1)S(1)}, bf16[576,128]{1,0:T(8,128)(2,1)S(1)}) custom-call(bf16[576,2048]{1,0:T(8,128)(2,1)} %bitcast.10, bf16[432,2048]{1,0:T(8,128)(2,1)} %bitcast.11, bf16[16,2048]{1,0:T(8,128)(2,1)} %bitcast.14, bf16[4,16,16,256]{3,2,1,0:T(8,128)(2,1)} %bitcast.12, bf16[576,256]{1,0:T(8,128)(2,1)} %bitcast.13, ...), custom_call_target="tpu_custom_call" | custom-call | tf_op jit(solution)/shard_map/pyramid/pallas_call | solution.py:475
  85.7 0.7 hand_out.1
